TPU v7x, 256 devices: a whole 4x4x8 slice. The times are simulated.
256 devices in a mesh: expert: 32 (over z, y), etp: 8 (over x, core).
Axes of the slice: x: 4, y: 4, z: 8, core: 2. Of those that a mesh axis runs over, the one named last changes fastest.
Arguments:
- tokens: bfloat16 [32768, 2560], P(('expert', 'etp')), may hold values from -6 to 6
- grad_out: bfloat16 [32768, 2560], P(('expert', 'etp')), may hold values from -6 to 6
- router_weight: bfloat16 [2560, 32], replicated, may hold values from -0.125 to 0.125
- expert_choice: int32 [32768, 1], P(('expert', 'etp')), may hold values from 0 to 31; in each aligned block of 128 rows (0 to 127, 128 to 255, ...) at most 6 rows name the same one
- gate_pre: bfloat16 [32, 1536, 4096], P('expert', None, 'etp'), may hold values from -6 to 6
- up_pre: bfloat16 [32, 1536, 4096], P('expert', None, 'etp'), may hold values from -6 to 6
- w_gate: bfloat16 [32, 2560, 4096], P('expert', None, 'etp'), may hold values from -0.125 to 0.125
- w_up: bfloat16 [32, 2560, 4096], P('expert', None, 'etp'), may hold values from -0.125 to 0.125
- w_down: bfloat16 [32, 4096, 2560], P('expert', 'etp'), may hold values from -0.09375 to 0.09375
Outputs:
- token_grad: bfloat16 [32768, 2560], P(('expert', 'etp'))
- router_grad: float32 [2560, 32], replicated
Inputs may be any that keep to these rules, and one draw needn't show every extreme that they name: `expert_choice`: within the 128 tokens of one device no expert is chosen more than 6 times, and in every draw some expert is chosen exactly 6 times by the tokens of some device.
All inputs are finite; a program needn't handle non-finite values.
Results may differ from a plain program's by a relative error of at most 0.015.
Values may be sent and summed in bfloat16 or wider, within the bound.
No kernel may reach another device: no remote copies, remote signals or barrier semaphores. Data moves between devices by JAX's collectives and lax.ppermute only.
A program may use at most 128 MiB of HBM per device.

v0:
```python
import jax
import jax.numpy as jnp
from jax import lax
from jax.sharding import PartitionSpec as P


def local(tokens, grad_out, router_weight, expert_choice, gate_pre, up_pre, w_gate, w_up, w_down):
    width = tokens.shape[1]
    experts = router_weight.shape[1]
    n_expert = lax.axis_size("expert")
    n_etp = lax.axis_size("etp")
    capacity = gate_pre.shape[1] // (n_expert * n_etp)
    contract = (((1,), (1,)), ((), ()))
    chosen_ids = expert_choice[:, 0]
    picked = chosen_ids[:, None] == jnp.arange(experts, dtype=jnp.int32)[None, :]
    logits = jnp.dot(tokens, router_weight, preferred_element_type=jnp.float32)
    score = jax.nn.sigmoid(jnp.sum(jnp.where(picked, logits, 0.0), axis=1))
    counts = picked.astype(jnp.int32)
    earlier = jnp.cumsum(counts, axis=0) - counts
    position = jnp.sum(earlier * counts, axis=1)
    target = chosen_ids * capacity + position
    placed = jnp.arange(experts * capacity, dtype=jnp.int32)[:, None] == target[None, :]
    onehot = placed.astype(jnp.bfloat16)
    outgoing = jnp.dot(onehot, grad_out, preferred_element_type=jnp.float32).astype(jnp.bfloat16)
    own = lax.all_to_all(outgoing, "expert", split_axis=0, concat_axis=0, tiled=True)
    arrived = lax.all_gather(own, "etp", axis=0, tiled=True)
    d_hidden = lax.dot_general(arrived, w_down[0], contract, preferred_element_type=jnp.float32)
    gate_f = gate_pre[0].astype(jnp.float32)
    up_f = up_pre[0].astype(jnp.float32)
    sig = jax.nn.sigmoid(gate_f)
    d_gate = (d_hidden * up_f * sig * (1.0 + gate_f * (1.0 - sig))).astype(jnp.bfloat16)
    d_up = (d_hidden * gate_f * sig).astype(jnp.bfloat16)
    terms = (
        lax.dot_general(d_gate, w_gate[0], contract, preferred_element_type=jnp.float32)
        + lax.dot_general(d_up, w_up[0], contract, preferred_element_type=jnp.float32)
    ).astype(jnp.bfloat16)
    summed = lax.psum_scatter(terms, "etp", scatter_dimension=0, tiled=True)
    returned = lax.all_to_all(summed, "expert", split_axis=0, concat_axis=0, tiled=True)
    fetched = lax.dot_general(
        onehot, returned, (((0,), (0,)), ((), ())), preferred_element_type=jnp.float32
    )
    inputs = tokens.astype(jnp.float32)
    d_logit = jnp.sum(inputs * fetched, axis=1) * score * (1.0 - score)
    column = lax.dot_general(
        picked.astype(jnp.bfloat16), router_weight, contract, preferred_element_type=jnp.float32
    )
    token_grad = (score[:, None] * fetched + d_logit[:, None] * column).astype(jnp.bfloat16)
    weighted = jnp.where(picked, d_logit[:, None], 0.0)
    local_terms = lax.dot_general(
        weighted,
        inputs,
        (((0,), (0,)), ((), ())),
        precision=lax.Precision.HIGHEST,
        preferred_element_type=jnp.float32,
    )
    mine = lax.all_to_all(
        local_terms.reshape(n_etp, experts // n_etp, width),
        "etp",
        split_axis=0,
        concat_axis=0,
        tiled=True,
    )
    mine = jnp.sum(mine, axis=0)
    mine = lax.psum(mine, "expert")
    router_grad = lax.all_gather(mine, "etp", axis=0, tiled=True).T
    return (token_grad, router_grad)


def solution(mesh):
    placed = (
        P(("expert", "etp"), None),
        P(("expert", "etp"), None),
        P(),
        P(("expert", "etp"), None),
        P("expert", None, "etp"),
        P("expert", None, "etp"),
        P("expert", None, "etp"),
        P("expert", None, "etp"),
        P("expert", "etp", None),
    )
    return jax.shard_map(
        local,
        mesh=mesh,
        in_specs=placed,
        out_specs=(P(("expert", "etp"), None), P()),
        check_vma=False,
    )
```

profile of v0, /device:TPU:1, one launch (start us, length us, event | category | flops | bytes accessed | tf_op | source)
XLA Modules:
  0.0 423.1 jit_solution(13606596880845416231)
XLA Ops:
  7.2 0.8 fusion.29
  9.7 2.5 convolution_convert_fusion
  12.2 2.3 all_to_all.19
  14.4 46.0 %all_to_all.29 = bf16[32,6,2560]{2,1,0:T(8,128)(2,1)} all-to-all(bf16[32,6,2560]{2,1,0:T(8,128)(2,1)} %all_to_all.19), channel_id=1, replica_groups=mesh['expert'=32,'etp'=8] {'expert'}, dimensions={0} | all-to-all | bytes 1966080 | tf_op jit(solution)/shard_map/all_to_all | solution.py:25
  60.4 2.3 all_to_all.21
  62.8 47.8 %all-gather.3.cloned.1.call-done = bf16[1536,2560]{1,0:T(8,128)(2,1)} async-done(((bf16[192,2560]{1,0:T(8,128)(2,1)}), bf16[1536,2560]{1,0:T(8,128)(2,1)}) %all-gather.3.cloned.1.call-update) | async-done | bytes 7864336 | tf_op jit(solution)/shard_map/all_gather | solution.py:26
  110.6 7.5 %fusion.14 = f32[1536,512]{1,0:T(8,128)S(1)} fusion(bf16[1536,2560]{1,0:T(8,128)(2,1)} %all-gather.3.cloned.1.call-done, bf16[1,512,2560]{2,1,0:T(8,128)(2,1)} %param.17), kind=kOutput, calls=%fused_computation.21 | convolution fusion | flops 4026531840 | bytes 13631488 | tf_op jit(solution)/shard_map/dot_general | solution.py:27
  118.1 1.7 copy-done.6
  119.8 9.8 %fusion.12 = f32[1536,2560]{1,0:T(8,128)} fusion(bf16[1,2560,512]{2,1,0:T(8,128)(2,1)S(1)} %copy-done, f32[1536,512]{1,0:T(8,128)S(1)} %fusion.14, bf16[1,1536,512]{2,1,0:T(8,128)(2,1)S(1)} %copy-done.4, bf16[1,1536,512]{2,1,0:T(8,128)(2,1)S(1)} %copy-done.5), kind=kOutput, calls=%fused_computation.19 | convolution fusion | flops 4035969024 | bytes 24641536 | tf_op jit(solution)/shard_map/dot_general | solution.py:34
  129.6 15.2 %add_convert_fusion = bf16[1536,2560]{1,0:T(8,128)(2,1)} fusion(f32[1536,2560]{1,0:T(8,128)} %fusion.12, bf16[1,2560,512]{2,1,0:T(8,128)(2,1)} %param.16, f32[1536,512]{1,0:T(8,128)} %copy-done.6, bf16[1,1536,512]{2,1,0:T(8,128)(2,1)} %param.13), kind=kOutput, calls=%fused_computation | convolution fusion | flops 4039901184 | bytes 30932992 | tf_op jit(solution)/shard_map/dot_general | solution.py:35
  144.9 51.8 %reduce-scatter.2.cloned.1.call-done = bf16[192,2560]{1,0:T(8,128)(2,1)} async-done(((bf16[1536,2560]{1,0:T(8,128)(2,1)}), bf16[192,2560]{1,0:T(8,128)(2,1)}) %reduce-scatter.2.cloned.1.call-update) | async-done | bytes 983056 | tf_op jit(solution)/shard_map/reduce_scatter | solution.py:37
  196.8 2.3 all_to_all.22
  199.0 9.7 %all-to-all-start.1 = ((bf16[32,6,2560]{2,1,0:T(8,128)(2,1)}), bf16[32,6,2560]{2,1,0:T(8,128)(2,1)}, u32[]{:S(2)}, u32[]{:S(2)}) async-start(bf16[32,6,2560]{2,1,0:T(8,128)(2,1)} %all_to_all.22), calls=%async_computation.2 | async-start | bytes 2621440 | tf_op jit(solution)/shard_map/all_to_all | solution.py:38
  209.1 30.4 %all-to-all-done.1 = bf16[32,6,2560]{2,1,0:T(8,128)(2,1)} async-done(((bf16[32,6,2560]{2,1,0:T(8,128)(2,1)}), bf16[32,6,2560]{2,1,0:T(8,128)(2,1)}, u32[]{:S(2)}, u32[]{:S(2)}) %all-to-all-start.1) | async-done | bytes 983072 | tf_op jit(solution)/shard_map/all_to_all | solution.py:38
  239.5 2.2 all_to_all.24
  241.7 2.7 multiply_reduce_fusion
  244.4 1.1 fusion.27
  245.5 1.8 reshape.36
  247.3 7.3 %all-to-all-start.2 = ((f32[8,4,2560]{2,1,0:T(4,128)}), f32[8,4,2560]{2,1,0:T(4,128)S(1)}, u32[]{:S(2)}, u32[]{:S(2)}) async-start(f32[8,4,2560]{2,1,0:T(4,128)} %reshape.36), calls=%async_computation.3 | async-start | bytes 655360 | tf_op jit(solution)/shard_map/all_to_all | solution.py:56
  254.6 2.5 fusion.1
  257.1 4.6 %all-to-all-done.2 = f32[8,4,2560]{2,1,0:T(4,128)S(1)} async-done(((f32[8,4,2560]{2,1,0:T(4,128)}), f32[8,4,2560]{2,1,0:T(4,128)S(1)}, u32[]{:S(2)}, u32[]{:S(2)}) %all-to-all-start.2) | async-done | bytes 327712 | tf_op jit(solution)/shard_map/all_to_all | solution.py:56
  261.8 112.4 %psum.7 = f32[4,2560]{1,0:T(4,128)S(1)} all-reduce(f32[4,2560]{1,0:T(4,128)S(1)} %reduce_sum.39), channel_id=1, replica_groups=mesh['expert'=32,'etp'=8] {'expert'}, use_global_device_ids=true, to_apply=%region_6.7 | all-reduce | flops 10240 | bytes 81920 | tf_op jit(solution)/shard_map/psum | solution.py:64
  374.2 41.3 %all-gather = f32[8,4,2560]{2,1,0:T(4,128)S(1)} all-gather(f32[1,4,2560]{2,1,0:T(4,128)S(1)} %bitcast.37), channel_id=1, replica_groups=mesh['expert'=32,'etp'=8] {'etp'}, dimensions={0}, use_global_device_ids=true | all-gather | bytes 368640 | tf_op jit(solution)/shard_map/all_gather | solution.py:65
  415.5 0.8 reshape.40
  (25 shorter events, 2.2 us)
Async XLA Ops:
  7.2 112.6 %copy-start = (bf16[1,2560,512]{2,1,0:T(8,128)(2,1)S(1)}, bf16[1,2560,512]{2,1,0:T(8,128)(2,1)}, u32[]{:S(2)}) copy-start(bf16[1,2560,512]{2,1,0:T(8,128)(2,1)} %param.15) | copy-start | bytes 7864324
  7.2 103.4 %all-gather.3.cloned.1.call-start = ((), (), s32[]{:S(2)}) async-start(), calls=%async_computation.4 | async-start | bytes 8847360 | tf_op jit(solution)/shard_map/all_gather | solution.py:26
  62.7 134.0 %reduce-scatter.2.cloned.1.call-start = ((), (), s32[]{:S(2)}) async-start(), calls=%async_computation.5 | async-start | bytes 8847360 | tf_op jit(solution)/shard_map/reduce_scatter | solution.py:37
  110.6 9.3 %copy-start.4 = (bf16[1,1536,512]{2,1,0:T(8,128)(2,1)S(1)}, bf16[1,1536,512]{2,1,0:T(8,128)(2,1)}, u32[]{:S(2)}) copy-start(bf16[1,1536,512]{2,1,0:T(8,128)(2,1)} %param.14) | copy-start | bytes 4718596
  110.6 9.3 %copy-start.5 = (bf16[1,1536,512]{2,1,0:T(8,128)(2,1)S(1)}, bf16[1,1536,512]{2,1,0:T(8,128)(2,1)}, u32[]{:S(2)}) copy-start(bf16[1,1536,512]{2,1,0:T(8,128)(2,1)} %param.13) | copy-start | bytes 4718596
  118.1 1.7 copy-start.6
  144.9 63.8 %copy-start.1 = (bf16[128,2560]{1,0:T(8,128)(2,1)S(1)}, bf16[128,2560]{1,0:T(8,128)(2,1)}, u32[]{:S(2)}) copy-start(bf16[128,2560]{1,0:T(8,128)(2,1)} %param.9) | copy-start | bytes 1966084
  144.9 63.8 %copy-start.2 = (bf16[2560,32]{0,1:T(8,128)(2,1)S(1)}, bf16[2560,32]{0,1:T(8,128)(2,1)}, u32[]{:S(2)}) copy-start(bf16[2560,32]{0,1:T(8,128)(2,1)} %param.11) | copy-start | bytes 491524
  144.9 63.8 %copy-start.3 = (s32[128,1]{0,1:T(1,128)S(1)}, s32[128,1]{0,1:T(1,128)}, u32[]{:S(2)}) copy-start(s32[128,1]{0,1:T(1,128)} %param.12) | copy-start | bytes 1540
  199.0 40.4 %all-to-all-start.1 = ((bf16[32,6,2560]{2,1,0:T(8,128)(2,1)}), bf16[32,6,2560]{2,1,0:T(8,128)(2,1)}, u32[]{:S(2)}, u32[]{:S(2)}) async-start(bf16[32,6,2560]{2,1,0:T(8,128)(2,1)} %all_to_all.22), calls=%async_computation.2 | async-start | bytes 2621440 | tf_op jit(solution)/shard_map/all_to_all | solution.py:38
  247.3 14.4 %all-to-all-start.2 = ((f32[8,4,2560]{2,1,0:T(4,128)}), f32[8,4,2560]{2,1,0:T(4,128)S(1)}, u32[]{:S(2)}, u32[]{:S(2)}) async-start(f32[8,4,2560]{2,1,0:T(4,128)} %reshape.36), calls=%async_computation.3 | async-start | bytes 655360 | tf_op jit(solution)/shard_map/all_to_all | solution.py:56
Sparse Core Ops, SparseCore 0:
  62.9 47.6 all-gather.2
  145.0 51.6 reduce-scatter.1
where the time goes:
time: 424 us; the launch traced here: 423 us
  blocking collectives  200 us (47%)
  waiting for transfers between devices  135 us (32%)
  matrix products  41.7 us (10%)
  starting transfers between devices  17.1 us (4%)
  between operations  14.1 us (3%)
  local copies, waits for them, and re-layouts  13.6 us (3%)
    psum x1, blocking collectives, local(): mine = lax.psum(mine, 'expert')  112 us
    reduce_scatter x1, waiting for transfers between devices, local(): summed = lax.psum_scatter(terms, 'etp', scatter_dimension=0, tiled=True)  51.8 us
    all_gather x1, waiting for transfers between devices, local(): arrived = lax.all_gather(own, 'etp', axis=0, tiled=True)  47.8 us
    all_to_all x1, blocking collectives, local(): lax.all_to_all(outgoing, 'expert', split_axis=0, concat_axis=0, tiled=True)  46 us
    all_gather x1, blocking collectives, local(): router_grad = lax.all_gather(mine, 'etp', axis=0, tiled=True).T  41.3 us
    all_to_all x1, waiting for transfers between devices, local(): lax.all_to_all(summed, 'expert', split_axis=0, concat_axis=0, tiled=True)  30.4 us
    dot_general x1, matrix products, local(): lax.dot_general(d_up, w_up[0], contract, preferred_element_type=jnp.float32)  15.2 us
    dot_general x1, matrix products, local(): lax.dot_general(d_gate, w_gate[0], contract, preferred_element_type=jnp.f...  9.81 us
  transfers between devices with their start and end apart: 4, of which 4 were waited for; matrix products, arithmetic and copies ran while one was open for 1% of the time, Pallas kernels for 0%

commit v1 on v0

--- a/solution.py
+++ b/solution.py
@@ -2,6 +2,8 @@
 import jax.numpy as jnp
 from jax import lax
 from jax.sharding import PartitionSpec as P
+
+face_touch = lambda view, shard_axis: jnp.sum(lax.all_gather(view, shard_axis), 0)
 
 
 def local(tokens, grad_out, router_weight, expert_choice, gate_pre, up_pre, w_gate, w_up, w_down):
@@ -61,7 +63,7 @@
         tiled=True,
     )
     mine = jnp.sum(mine, axis=0)
-    mine = lax.psum(mine, "expert")
+    mine = face_touch(mine, "expert")
     router_grad = lax.all_gather(mine, "etp", axis=0, tiled=True).T
     return (token_grad, router_grad)
 

time: 424 us -> 357 us (0.84)
  blocking collectives: 200 us -> 78.7 us
  waiting for transfers between devices: 135 us -> 195 us
  starting transfers between devices: 17.1 us -> 9.81 us
    psum x1 -> x0, blocking collectives: 112 us -> none  [local(): mine = lax.psum(mine, 'expert')]
    all_gather x0 -> x1, waiting for transfers between devices: none -> 64.9 us  [lax.all_gather(view, shard_axis)]
    all_gather x1, blocking collectives: 41.3 us -> 18.1 us  [local(): router_grad = lax.all_gather(mine, 'etp', axis=0, tiled=True).T]
    all_to_all x0 -> x1, blocking collectives: none -> 14.6 us  [local(): lax.all_to_all(local_terms.reshape(n_etp, experts // n_etp, width), 'etp'...]
    all_to_all x1 -> x0, starting transfers between devices: 7.3 us -> none  [local(): lax.all_to_all(local_terms.reshape(n_etp, experts // n_etp, width), 'etp'...]
    all_to_all x1 -> x0, waiting for transfers between devices: 4.58 us -> none  [local(): lax.all_to_all(local_terms.reshape(n_etp, experts // n_etp, width), 'etp'...]
where the time goes in v1:
time: 357 us; the launch traced here: 356 us
  waiting for transfers between devices  195 us (55%)
  blocking collectives  78.7 us (22%)
  matrix products  41.7 us (12%)
  between operations  13.8 us (4%)
  local copies, waits for them, and re-layouts  12.9 us (4%)
  starting transfers between devices  9.81 us (3%)
  other arithmetic  4.55 us (1%)
    all_gather x1, waiting for transfers between devices, lax.all_gather(view, shard_axis)  64.9 us
    reduce_scatter x1, waiting for transfers between devices, local(): summed = lax.psum_scatter(terms, 'etp', scatter_dimension=0, tiled=True)  51.8 us
    all_gather x1, waiting for transfers between devices, local(): arrived = lax.all_gather(own, 'etp', axis=0, tiled=True)  47.8 us
    all_to_all x1, blocking collectives, local(): lax.all_to_all(outgoing, 'expert', split_axis=0, concat_axis=0, tiled=True)  46 us
    all_to_all x1, waiting for transfers between devices, local(): lax.all_to_all(summed, 'expert', split_axis=0, concat_axis=0, tiled=True)  30.3 us
    all_gather x1, blocking collectives, local(): router_grad = lax.all_gather(mine, 'etp', axis=0, tiled=True).T  18.1 us
    dot_general x1, matrix products, local(): lax.dot_general(d_up, w_up[0], contract, preferred_element_type=jnp.float32)  15.2 us
    all_to_all x1, blocking collectives, local(): lax.all_to_all(local_terms.reshape(n_etp, experts // n_etp, width), 'etp'...  14.6 us
  transfers between devices with their start and end apart: 4, of which 4 were waited for; matrix products, arithmetic and copies ran while one was open for 1% of the time, Pallas kernels for 0%

profile of v1, /device:TPU:1, one launch (start us, length us, event | category | flops | bytes accessed | tf_op | source)
XLA Modules:
  0.0 356.3 jit_solution(13958498987821106013)
XLA Ops:
  7.2 0.8 fusion.29
  9.7 2.5 convolution_convert_fusion
  12.2 2.3 all_to_all.19
  14.4 46.0 %all_to_all.29 = bf16[32,6,2560]{2,1,0:T(8,128)(2,1)} all-to-all(bf16[32,6,2560]{2,1,0:T(8,128)(2,1)} %all_to_all.19), channel_id=1, replica_groups=mesh['expert'=32,'etp'=8] {'expert'}, dimensions={0} | all-to-all | bytes 1966080 | tf_op jit(solution)/shard_map/all_to_all | solution.py:27
  60.4 2.3 all_to_all.21
  62.8 47.8 %all-gather.6.cloned.1.call-done = bf16[1536,2560]{1,0:T(8,128)(2,1)} async-done(((bf16[192,2560]{1,0:T(8,128)(2,1)}), bf16[1536,2560]{1,0:T(8,128)(2,1)}) %all-gather.6.cloned.1.call-update) | async-done | bytes 7864336 | tf_op jit(solution)/shard_map/all_gather | solution.py:28
  110.6 7.5 %fusion.14 = f32[1536,512]{1,0:T(8,128)S(1)} fusion(bf16[1536,2560]{1,0:T(8,128)(2,1)} %all-gather.6.cloned.1.call-done, bf16[1,512,2560]{2,1,0:T(8,128)(2,1)} %param.17), kind=kOutput, calls=%fused_computation.21 | convolution fusion | flops 4026531840 | bytes 13631488 | tf_op jit(solution)/shard_map/dot_general | solution.py:29
  118.1 1.7 copy-done.6
  119.8 9.8 %fusion.12 = f32[1536,2560]{1,0:T(8,128)} fusion(bf16[1,2560,512]{2,1,0:T(8,128)(2,1)S(1)} %copy-done, f32[1536,512]{1,0:T(8,128)S(1)} %fusion.14, bf16[1,1536,512]{2,1,0:T(8,128)(2,1)S(1)} %copy-done.4, bf16[1,1536,512]{2,1,0:T(8,128)(2,1)S(1)} %copy-done.5), kind=kOutput, calls=%fused_computation.19 | convolution fusion | flops 4035969024 | bytes 24641536 | tf_op jit(solution)/shard_map/dot_general | solution.py:36
  129.6 15.2 %add_convert_fusion = bf16[1536,2560]{1,0:T(8,128)(2,1)} fusion(f32[1536,2560]{1,0:T(8,128)} %fusion.12, bf16[1,2560,512]{2,1,0:T(8,128)(2,1)} %param.16, f32[1536,512]{1,0:T(8,128)} %copy-done.6, bf16[1,1536,512]{2,1,0:T(8,128)(2,1)} %param.13), kind=kOutput, calls=%fused_computation | convolution fusion | flops 4039901184 | bytes 30932992 | tf_op jit(solution)/shard_map/dot_general | solution.py:37
  144.9 51.8 %reduce-scatter.2.cloned.1.call-done = bf16[192,2560]{1,0:T(8,128)(2,1)} async-done(((bf16[1536,2560]{1,0:T(8,128)(2,1)}), bf16[192,2560]{1,0:T(8,128)(2,1)}) %reduce-scatter.2.cloned.1.call-update) | async-done | bytes 983056 | tf_op jit(solution)/shard_map/reduce_scatter | solution.py:39
  196.8 2.3 all_to_all.22
  199.0 9.7 %all-to-all-start.1 = ((bf16[32,6,2560]{2,1,0:T(8,128)(2,1)}), bf16[32,6,2560]{2,1,0:T(8,128)(2,1)}, u32[]{:S(2)}, u32[]{:S(2)}) async-start(bf16[32,6,2560]{2,1,0:T(8,128)(2,1)} %all_to_all.22), calls=%async_computation.2 | async-start | bytes 2621440 | tf_op jit(solution)/shard_map/all_to_all | solution.py:40
  209.1 30.3 %all-to-all-done.1 = bf16[32,6,2560]{2,1,0:T(8,128)(2,1)} async-done(((bf16[32,6,2560]{2,1,0:T(8,128)(2,1)}), bf16[32,6,2560]{2,1,0:T(8,128)(2,1)}, u32[]{:S(2)}, u32[]{:S(2)}) %all-to-all-start.1) | async-done | bytes 983072 | tf_op jit(solution)/shard_map/all_to_all | solution.py:40
  239.5 2.2 all_to_all.24
  241.7 2.7 multiply_reduce_fusion
  244.4 1.1 fusion.27
  245.5 1.1 reshape.36
  246.5 14.6 %all_to_all.30 = f32[8,4,2560]{2,1,0:T(4,128)S(1)} all-to-all(f32[8,4,2560]{2,1,0:T(4,128)S(1)} %reshape.36), channel_id=1, replica_groups=mesh['expert'=32,'etp'=8] {'etp'}, dimensions={0} | all-to-all | bytes 655360 | tf_op jit(solution)/shard_map/all_to_all | solution.py:58
  261.8 2.5 fusion.1
  264.4 64.9 %all-gather.8.cloned.1.call-done = f32[32,4,2560]{2,1,0:T(4,128)} async-done(((f32[1,4,2560]{2,1,0:T(4,128)}), f32[32,4,2560]{2,1,0:T(4,128)}) %all-gather.8.cloned.1.call-update) | async-done | bytes 1310736 | tf_op jit(solution)/shard_map/all_gather | solution.py:6
  329.3 1.5 reduce_sum.49
  330.8 18.1 %all-gather.2 = f32[8,4,2560]{2,1,0:T(4,128)S(1)} all-gather(f32[1,4,2560]{2,1,0:T(4,128)S(1)} %bitcast.38), channel_id=1, replica_groups=mesh['expert'=32,'etp'=8] {'etp'}, dimensions={0}, use_global_device_ids=true | all-gather | bytes 368640 | tf_op jit(solution)/shard_map/all_gather | solution.py:67
  349.0 0.8 reshape.43
  (27 shorter events, 2.9 us)
Async XLA Ops:
  7.2 112.6 %copy-start = (bf16[1,2560,512]{2,1,0:T(8,128)(2,1)S(1)}, bf16[1,2560,512]{2,1,0:T(8,128)(2,1)}, u32[]{:S(2)}) copy-start(bf16[1,2560,512]{2,1,0:T(8,128)(2,1)} %param.15) | copy-start | bytes 7864324
  7.2 103.4 %all-gather.6.cloned.1.call-start = ((), (), s32[]{:S(2)}) async-start(), calls=%async_computation.4 | async-start | bytes 8847360 | tf_op jit(solution)/shard_map/all_gather | solution.py:28
  62.7 134.0 %reduce-scatter.2.cloned.1.call-start = ((), (), s32[]{:S(2)}) async-start(), calls=%async_computation.5 | async-start | bytes 8847360 | tf_op jit(solution)/shard_map/reduce_scatter | solution.py:39
  110.6 9.3 %copy-start.4 = (bf16[1,1536,512]{2,1,0:T(8,128)(2,1)S(1)}, bf16[1,1536,512]{2,1,0:T(8,128)(2,1)}, u32[]{:S(2)}) copy-start(bf16[1,1536,512]{2,1,0:T(8,128)(2,1)} %param.14) | copy-start | bytes 4718596
  110.6 9.3 %copy-start.5 = (bf16[1,1536,512]{2,1,0:T(8,128)(2,1)S(1)}, bf16[1,1536,512]{2,1,0:T(8,128)(2,1)}, u32[]{:S(2)}) copy-start(bf16[1,1536,512]{2,1,0:T(8,128)(2,1)} %param.13) | copy-start | bytes 4718596
  118.1 1.7 copy-start.6
  144.9 63.9 %copy-start.1 = (bf16[128,2560]{1,0:T(8,128)(2,1)S(1)}, bf16[128,2560]{1,0:T(8,128)(2,1)}, u32[]{:S(2)}) copy-start(bf16[128,2560]{1,0:T(8,128)(2,1)} %param.9) | copy-start | bytes 1966084
  144.9 63.9 %copy-start.2 = (bf16[2560,32]{0,1:T(8,128)(2,1)S(1)}, bf16[2560,32]{0,1:T(8,128)(2,1)}, u32[]{:S(2)}) copy-start(bf16[2560,32]{0,1:T(8,128)(2,1)} %param.11) | copy-start | bytes 491524
  144.9 63.9 %copy-start.3 = (s32[128,1]{0,1:T(1,128)S(1)}, s32[128,1]{0,1:T(1,128)}, u32[]{:S(2)}) copy-start(s32[128,1]{0,1:T(1,128)} %param.12) | copy-start | bytes 1540
  199.0 40.4 %all-to-all-start.1 = ((bf16[32,6,2560]{2,1,0:T(8,128)(2,1)}), bf16[32,6,2560]{2,1,0:T(8,128)(2,1)}, u32[]{:S(2)}, u32[]{:S(2)}) async-start(bf16[32,6,2560]{2,1,0:T(8,128)(2,1)} %all_to_all.22), calls=%async_computation.2 | async-start | bytes 2621440 | tf_op jit(solution)/shard_map/all_to_all | solution.py:40
  208.7 120.6 %all-gather.8.cloned.1.call-start = ((), (), s32[]{:S(2)}) async-start(), calls=%async_computation.6 | async-start | bytes 1351680 | tf_op jit(solution)/shard_map/all_gather | solution.py:6
Sparse Core Ops, SparseCore 0:
  62.9 47.6 all-gather.5
  145.0 51.6 reduce-scatter.1
  262.0 67.2 all-gather.7
